TPU v7x, 256 devices: a whole 4x4x8 slice. The times are simulated.
256 devices in a mesh: chan: 2 (over x_lo), elem: 8 (over y, x_hi), beam: 16 (over z, core).
Axes of the slice: x: 4 (x_hi: 2, x_lo: 2; x = x_hi * 2 + x_lo), y: 4, z: 8, core: 2. Of those that a mesh axis runs over, the one named last changes fastest.
Arguments:
- voltages: bfloat16 [2, 128, 256, 2048], P(None, 'chan', 'beam', 'elem'), may hold values from -6 to 6
- weights: bfloat16 [2, 128, 2048, 2048], P(None, 'chan', 'elem', 'beam'), may hold values from -0.09375 to 0.09375
Outputs:
- power: float32 [128, 256, 2048], P(None, ('chan', 'elem'), 'beam')
All inputs are finite; a program needn't handle non-finite values.
Results may differ from a plain program's by a relative error of at most 0.012.
Values may be sent and summed in bfloat16 or wider, within the bound.
A program may use at most 128 MiB of HBM per device.

v0:
```python
import jax
import jax.numpy as jnp
from jax import lax
from jax.sharding import PartitionSpec as P


def dft_tables(channels):
    index = jnp.arange(channels, dtype=jnp.int32)
    phase = index[:, None] * index[None, :] % channels
    angle = phase.astype(jnp.float32) * (2.0 * jnp.pi / channels)
    factor = 1.0 / jnp.sqrt(jnp.float32(channels))
    return (jnp.cos(angle) * factor, jnp.sin(angle) * factor)


def shards(voltages, weights):
    local_beams = weights.shape[3]
    volt_piece = lax.all_gather(voltages, "beam", axis=2, tiled=True)
    real_part = jnp.einsum(
        "cte,ceb->ctb", volt_piece[0], weights[0], preferred_element_type=jnp.float32
    ) - jnp.einsum("cte,ceb->ctb", volt_piece[1], weights[1], preferred_element_type=jnp.float32)
    imag_part = jnp.einsum(
        "cte,ceb->ctb", volt_piece[0], weights[1], preferred_element_type=jnp.float32
    ) + jnp.einsum("cte,ceb->ctb", volt_piece[1], weights[0], preferred_element_type=jnp.float32)
    partial_value = jnp.stack([real_part, imag_part])
    summed = lax.psum_scatter(
        partial_value.astype(jnp.bfloat16), "elem", scatter_dimension=1, tiled=True
    )
    owned = lax.all_to_all(summed, ("chan", "elem"), split_axis=2, concat_axis=1, tiled=True)
    channels = owned.shape[1]
    own_time = owned.shape[2]
    cosine, sine = dft_tables(channels)
    real_in = owned[0].astype(jnp.float32).reshape(channels, own_time * local_beams)
    imag_in = owned[1].astype(jnp.float32).reshape(channels, own_time * local_beams)
    highest = lax.Precision.HIGHEST
    real_out = jnp.dot(
        cosine, real_in, precision=highest, preferred_element_type=jnp.float32
    ) - jnp.dot(sine, imag_in, precision=highest, preferred_element_type=jnp.float32)
    imag_out = jnp.dot(
        sine, real_in, precision=highest, preferred_element_type=jnp.float32
    ) + jnp.dot(cosine, imag_in, precision=highest, preferred_element_type=jnp.float32)
    power = real_out * real_out + imag_out * imag_out
    return power.reshape(channels, own_time, local_beams)


def solution(mesh):
    placed = (P(None, "chan", "beam", "elem"), P(None, "chan", "elem", "beam"))
    return jax.shard_map(
        shards,
        mesh=mesh,
        in_specs=placed,
        out_specs=P(None, ("chan", "elem"), "beam"),
        check_vma=False,
    )
```

profile of v0, /device:TPU:32, one launch (start us, length us, event | category | flops | bytes accessed | tf_op | source)
XLA Modules:
  0.0 328.4 jit_solution(3343616162390138863)
XLA Ops:
  6.5 0.0 all-gather.2.cloned.1.call-start
  6.5 0.7 all-gather.2.cloned.1.call-update
  7.3 0.0 reduce-scatter.5.cloned.1.call-start
  7.3 97.9 %all-gather.2.cloned.1.call-done = bf16[2,64,256,256]{3,2,1,0:T(8,128)(2,1)} async-done(((bf16[2,64,16,256]{3,2,1,0:T(8,128)(2,1)}), bf16[2,64,256,256]{3,2,1,0:T(8,128)(2,1)}) %all-gather.2.cloned.1.call-update) | async-done | bytes 16777232 | tf_op jit(solution)/shard_map/all_gather | solution.py:17
  105.2 10.1 %fusion = f32[64,256,128]{2,1,0:T(8,128)} fusion(bf16[2,64,256,256]{3,2,1,0:T(8,128)(2,1)} %all-gather.2.cloned.1.call-done, bf16[2,64,256,128]{3,2,1,0:T(8,128)(2,1)} %param.3), kind=kOutput, calls=%fused_computation.6 | convolution fusion | flops 1073741824 | bytes 20971520 | tf_op jit(solution)/shard_map/cte,ceb->ctb/dot_general | solution.py:21
  115.4 10.1 %fusion.1 = f32[64,256,128]{2,1,0:T(8,128)} fusion(bf16[2,64,256,256]{3,2,1,0:T(8,128)(2,1)} %all-gather.2.cloned.1.call-done, bf16[2,64,256,128]{3,2,1,0:T(8,128)(2,1)} %param.3), kind=kOutput, calls=%fused_computation.7 | convolution fusion | flops 1073741824 | bytes 20971520 | tf_op jit(solution)/shard_map/cte,ceb->ctb/dot_general | solution.py:18
  125.5 11.4 %fusion.5 = bf16[1,64,256,128]{3,2,1,0:T(8,128)(2,1)} fusion(f32[64,256,128]{2,1,0:T(8,128)} %fusion, bf16[2,64,256,128]{3,2,1,0:T(8,128)(2,1)} %param.3, bf16[2,64,256,256]{3,2,1,0:T(8,128)(2,1)} %all-gather.2.cloned.1.call-done), kind=kOutput, calls=%fused_computation.11 | convolution fusion | flops 1077936128 | bytes 25165824 | tf_op jit(solution)/shard_map/cte,ceb->ctb/dot_general | solution.py:23
  136.9 11.3 %fusion.4 = bf16[1,64,256,128]{3,2,1,0:T(8,128)(2,1)} fusion(f32[64,256,128]{2,1,0:T(8,128)} %fusion.1, bf16[2,64,256,128]{3,2,1,0:T(8,128)(2,1)} %param.3, bf16[2,64,256,256]{3,2,1,0:T(8,128)(2,1)} %all-gather.2.cloned.1.call-done), kind=kOutput, calls=%fused_computation.10 | convolution fusion | flops 1077936128 | bytes 25165824 | tf_op jit(solution)/shard_map/cte,ceb->ctb/dot_general | solution.py:20
  148.2 7.4 %pad_maximum_fusion = bf16[2,64,256,128]{3,2,1,0:T(8,128)(2,1)} fusion(bf16[1,64,256,128]{3,2,1,0:T(8,128)(2,1)} %fusion.5, bf16[1,64,256,128]{3,2,1,0:T(8,128)(2,1)} %fusion.4), kind=kLoop, calls=%fused_computation.3 | loop fusion | flops 4194304 | bytes 16777216 | tf_op jit(solution)/shard_map/stack | solution.py:24
  155.7 7.7 %copy.6 = bf16[2,64,256,128]{3,2,0,1:T(8,128)(2,1)} copy(bf16[2,64,256,128]{3,2,1,0:T(8,128)(2,1)} %pad_maximum_fusion) | data formatting | bytes 16777216
  163.4 12.2 %copy.33 = bf16[8,8,512,128]{3,1,2,0:T(8,128)(2,1)} copy(bf16[8,8,512,128]{3,2,1,0:T(8,128)(2,1)} %bitcast.69) | data formatting | bytes 16777216
  175.6 0.0 reduce-scatter.5.cloned.1.call-update
  175.6 120.1 %reduce-scatter.5.cloned.1.call-done = bf16[8,65536]{1,0:T(8,128)(2,1)} async-done(((bf16[64,65536]{1,0:T(8,128)(2,1)}), bf16[8,65536]{1,0:T(8,128)(2,1)}) %reduce-scatter.5.cloned.1.call-update) | async-done | bytes 1048592
  295.7 1.4 copy.4
  297.1 19.2 %all_to_all.15 = bf16[2,8,256,128]{3,1,0,2:T(8,128)(2,1)S(1)} all-to-all(bf16[2,8,256,128]{3,1,0,2:T(8,128)(2,1)S(1)} %copy.4), channel_id=1, replica_groups=mesh['chan'=2,'elem'=8,'beam'=16] {'chan','elem'}, dimensions={2} | all-to-all | bytes 2097152 | tf_op jit(solution)/shard_map/all_to_all | solution.py:28
  316.4 0.3 copy.34
  316.7 0.3 slice_bitcast_fusion.10
  316.9 0.8 fusion.24
  317.8 0.8 fusion.26
  318.6 0.8 fusion.16
  319.5 0.9 fusion.21
  320.4 1.2 copy.13
Async XLA Ops:
  6.5 98.7 %all-gather.2.cloned.1.call-start = ((), (), s32[]{:S(2)}) async-start(), calls=%async_computation.2 | async-start | bytes 17825792 | tf_op jit(solution)/shard_map/all_gather | solution.py:17
  7.3 288.5 %reduce-scatter.5.cloned.1.call-start = ((), (), s32[]{:S(2)}) async-start(), calls=%async_computation.3 | async-start | bytes 9437184
Sparse Core Ops, SparseCore 0:
  9.2 96.0 all-gather.1
  175.7 119.9 reduce-scatter.4
where the time goes:
time: 329 us; the launch traced here: 328 us
  waiting for transfers between devices  219 us (67%)
  matrix products  46.4 us (14%)
  local copies, waits for them, and re-layouts  23 us (7%)
  blocking collectives  19.2 us (6%)
  between operations  13.4 us (4%)
  other arithmetic  7.45 us (2%)
    unnamed x3, waiting for transfers between devices  121 us
    all_gather x1, waiting for transfers between devices, shards(): volt_piece = lax.all_gather(voltages, 'beam', axis=2, tiled=True)  97.9 us
    unnamed x4, local copies, waits for them, and re-layouts  21.3 us
    all_to_all x1, blocking collectives, shards(): lax.all_to_all(summed, ('chan', 'elem'), split_axis=2, concat_axis=1, til...  19.2 us
    dot_general x1, matrix products, shards(): jnp.einsum('cte,ceb->ctb', volt_piece[1], weights[0], preferred_element_t...  11.4 us
    dot_general x1, matrix products, shards(): jnp.einsum('cte,ceb->ctb', volt_piece[1], weights[1], preferred_element_t...  11.3 us
    dot_general x1, matrix products, shards(): jnp.einsum('cte,ceb->ctb', volt_piece[0], weights[0], preferred_element_t...  10.1 us
    dot_general x1, matrix products, shards(): jnp.einsum('cte,ceb->ctb', volt_piece[0], weights[1], preferred_element_t...  10.1 us
  transfers between devices with their start and end apart: 2, of which 2 were waited for; matrix products, arithmetic and copies ran while one was open for 0% of the time, Pallas kernels for 0%

commit v1 on v0

--- a/solution.py
+++ b/solution.py
@@ -14,7 +14,9 @@
 
 def shards(voltages, weights):
     local_beams = weights.shape[3]
-    volt_piece = lax.all_gather(voltages, "beam", axis=2, tiled=True)
+    volt_piece = jnp.concatenate(
+        lax.all_to_all(jnp.stack([voltages] * lax.axis_size("beam")), "beam", 0, 0), axis=2
+    )
     real_part = jnp.einsum(
         "cte,ceb->ctb", volt_piece[0], weights[0], preferred_element_type=jnp.float32
     ) - jnp.einsum("cte,ceb->ctb", volt_piece[1], weights[1], preferred_element_type=jnp.float32)

time: 329 us -> 618 us (1.88)
  blocking collectives: 19.2 us -> 390 us
  waiting for transfers between devices: 219 us -> 120 us
  local copies, waits for them, and re-layouts: 23 us -> 48.5 us
  matrix products: 46.4 us -> 39.9 us
    all_to_all x0 -> x1, blocking collectives: none -> 371 us  [shards(): lax.all_to_all(jnp.stack([voltages] * lax.axis_size('beam')), 'beam', 0, 0)]
    all_gather x1 -> x0, waiting for transfers between devices: 97.9 us -> none  [shards(): volt_piece = lax.all_gather(voltages, 'beam', axis=2, tiled=True)]
    slice x0 -> x3, local copies, waits for them, and re-layouts: none -> 21.8 us  [the longest x2 13.8 us: shards(): volt_piece[1]]
    unnamed x3 -> x2, waiting for transfers between devices: 121 us -> 120 us
    unnamed x4 -> x10, local copies, waits for them, and re-layouts: 21.3 us -> 21.4 us
  transfers between devices with their start and end apart: 2 -> 1, of which waited for: 2 -> 1; matrix products, arithmetic and copies ran while one was open for 0% -> 0% of each run, Pallas kernels for 0% -> 0%
where the time goes in v1:
time: 618 us
  blocking collectives  390 us (63%)
  waiting for transfers between devices  120 us (19%)
  local copies, waits for them, and re-layouts  48.5 us (8%)
  matrix products  39.9 us (6%)
  between operations  13.5 us (2%)
  other arithmetic  6.19 us (1%)
    all_to_all x1, blocking collectives, shards(): lax.all_to_all(jnp.stack([voltages] * lax.axis_size('beam')), 'beam', 0, 0)  371 us
    unnamed x2, waiting for transfers between devices  120 us
    unnamed x10, local copies, waits for them, and re-layouts  21.4 us
    all_to_all x1, blocking collectives, shards(): lax.all_to_all(summed, ('chan', 'elem'), split_axis=2, concat_axis=1, til...  19.3 us
    slice x2, local copies, waits for them, and re-layouts, shards(): volt_piece[1]  13.8 us
  transfers between devices with their start and end apart: 1, of which 1 were waited for; matrix products, arithmetic and copies ran while one was open for 0% of the time, Pallas kernels for 0%

profile of v1, /device:TPU:32, one launch (start us, length us, event | category | flops | bytes accessed | tf_op | source)
XLA Modules:
  0.0 617.9 jit_solution(3502128271423559940)
XLA Ops:
  6.5 0.0 reduce-scatter.5.cloned.1.call-start
  6.5 3.6 stack.11
  10.2 370.9 %all_to_all.20 = bf16[16,2,64,16,256]{4,3,2,1,0:T(8,128)(2,1)S(1)} all-to-all(bf16[16,2,64,16,256]{4,3,2,1,0:T(8,128)(2,1)S(1)} %stack.11), channel_id=1, replica_groups=mesh['chan'=2,'elem'=8,'beam'=16] {'beam'}, dimensions={0} | all-to-all | bytes 33554432 | tf_op jit(solution)/shard_map/all_to_all | solution.py:18
  381.1 6.0 fusion.66
  387.1 7.9 %copy.5 = bf16[1,64,16,16,256]{4,3,2,1,0:T(8,128)(2,1)} copy(bf16[1,64,16,16,256]{4,3,1,0,2:T(8,128)(2,1)} %get-tuple-element.5) | data formatting | bytes 16777216 | tf_op jit(solution)/shard_map/slice | solution.py:22
  394.9 0.0 slice-start
  394.9 8.0 %copy.4 = bf16[1,64,16,16,256]{4,3,2,1,0:T(8,128)(2,1)} copy(bf16[1,64,16,16,256]{4,3,1,0,2:T(8,128)(2,1)} %get-tuple-element.6) | data formatting | bytes 16777216 | tf_op jit(solution)/shard_map/slice | solution.py:21
  402.9 0.0 copy-start
  402.9 0.0 slice-start.1
  402.9 10.3 %fusion.4 = f32[64,256,128]{2,1,0:T(8,128)} fusion(bf16[64,256,256]{2,1,0:T(8,128)(2,1)} %bitcast.63, bf16[2,64,256,128]{3,2,1,0:T(8,128)(2,1)} %param.3), kind=kOutput, calls=%fused_computation.8 | convolution fusion | flops 1073741824 | bytes 20971520 | tf_op jit(solution)/shard_map/cte,ceb->ctb/dot_general | solution.py:22
  413.2 0.0 slice-done
  413.2 0.0 copy-done
  413.2 0.0 slice-done.1
  413.2 5.6 fusion.2
  418.8 9.4 %fusion = bf16[1,64,256,128]{3,2,1,0:T(8,128)(2,1)S(1)} fusion(f32[64,256,128]{2,1,0:T(8,128)} %fusion.4, bf16[64,256,256]{2,1,0:T(8,128)(2,1)} %bitcast.65, bf16[2,64,256,128]{3,2,1,0:T(8,128)(2,1)} %param.3), kind=kOutput, calls=%fused_computation.4 | convolution fusion | flops 1077936128 | bytes 25165824 | tf_op jit(solution)/shard_map/cte,ceb->ctb/dot_general | solution.py:20
  428.2 11.3 %fusion.1 = bf16[1,64,256,128]{3,2,1,0:T(8,128)(2,1)} fusion(f32[64,256,128]{2,1,0:T(8,128)} %fusion.2, bf16[64,256,256]{2,1,0:T(8,128)(2,1)} %bitcast.64, bf16[2,64,256,128]{3,2,1,0:T(8,128)(2,1)} %param.3), kind=kOutput, calls=%fused_computation.5 | convolution fusion | flops 1077936128 | bytes 25165824 | tf_op jit(solution)/shard_map/cte,ceb->ctb/dot_general | solution.py:25
  439.5 6.2 %pad_maximum_fusion = bf16[2,64,256,128]{3,2,1,0:T(8,128)(2,1)} fusion(bf16[1,64,256,128]{3,2,1,0:T(8,128)(2,1)} %fusion.1, bf16[1,64,256,128]{3,2,1,0:T(8,128)(2,1)S(1)} %fusion), kind=kLoop, calls=%fused_computation.1 | loop fusion | flops 4194304 | bytes 16777216 | tf_op jit(solution)/shard_map/stack | solution.py:26
  445.7 7.9 %copy.8 = bf16[2,64,256,128]{3,2,0,1:T(8,128)(2,1)} copy(bf16[2,64,256,128]{3,2,1,0:T(8,128)(2,1)} %pad_maximum_fusion) | data formatting | bytes 16777216
  453.6 12.0 %copy.35 = bf16[8,8,512,128]{3,1,2,0:T(8,128)(2,1)} copy(bf16[8,8,512,128]{3,2,1,0:T(8,128)(2,1)} %bitcast.71) | data formatting | bytes 16777216
  465.6 0.0 reduce-scatter.5.cloned.1.call-update
  465.6 119.6 %reduce-scatter.5.cloned.1.call-done = bf16[8,65536]{1,0:T(8,128)(2,1)} async-done(((bf16[64,65536]{1,0:T(8,128)(2,1)}), bf16[8,65536]{1,0:T(8,128)(2,1)}) %reduce-scatter.5.cloned.1.call-update) | async-done | bytes 1048592
  585.2 1.4 copy.6
  586.6 19.3 %all_to_all.21 = bf16[2,8,256,128]{3,1,0,2:T(8,128)(2,1)S(1)} all-to-all(bf16[2,8,256,128]{3,1,0,2:T(8,128)(2,1)S(1)} %copy.6), channel_id=1, replica_groups=mesh['chan'=2,'elem'=8,'beam'=16] {'chan','elem'}, dimensions={2} | all-to-all | bytes 2097152 | tf_op jit(solution)/shard_map/all_to_all | solution.py:30
  605.9 0.3 copy.36
  606.1 0.3 slice_bitcast_fusion
  606.4 0.8 fusion.24
  607.3 0.8 fusion.26
  608.1 0.8 fusion.20
  609.0 0.9 fusion.21
  609.9 1.2 copy.15
  (1 shorter events, 0.0 us)
Async XLA Ops:
  6.5 578.7 %reduce-scatter.5.cloned.1.call-start = ((), (), s32[]{:S(2)}) async-start(), calls=%async_computation.3 | async-start | bytes 9437184
  394.9 18.3 %slice-start = ((s8[8388608]{0:T(1024)(128)(4,1)}), s8[4194304]{0:T(1024)(128)(4,1)S(1)}, s32[]{:S(2)}) async-start(s8[8388608]{0:T(1024)(128)(4,1)} %bitcast.68), calls=%async_computation.4 | async-start | bytes 8388608
  402.9 10.3 %copy-start = (bf16[1,64,16,16,256]{4,3,2,1,0:T(8,128)(2,1)S(1)}, bf16[1,64,16,16,256]{4,3,2,1,0:T(8,128)(2,1)}, u32[]{:S(2)}) copy-start(bf16[1,64,16,16,256]{4,3,2,1,0:T(8,128)(2,1)} %copy.4) | copy-start | bytes 25165828
  402.9 10.3 %slice-start.1 = ((s8[8388608]{0:T(1024)(128)(4,1)}), s8[4194304]{0:T(1024)(128)(4,1)S(1)}, s32[]{:S(2)}) async-start(s8[8388608]{0:T(1024)(128)(4,1)} %bitcast.68), calls=%async_computation.5 | async-start | bytes 8388608
Sparse Core Ops, SparseCore 0:
  465.7 119.4 reduce-scatter.4
